TPU v7x, 32 devices: a whole 2x2x4 slice. The times are simulated.
32 devices in a mesh: gx: 16 (over z, x, core), yz: 2 (over y).
Axes of the slice: x: 2, y: 2, z: 4, core: 2. Of those that a mesh axis runs over, the one named last changes fastest.
Arguments:
- fields: float32 [5, 256, 512], P(None, 'gx', 'yz'), may hold values from 0.03 to 25, as said below
- node_cell: int32 [256, 512], P('gx', 'yz'), may hold values from 0 to 255, as said below
- node_frac: float32 [256, 512], P('gx', 'yz'), as said below
Outputs:
- remapped: float32 [5, 256, 512], P(None, 'gx', 'yz')
- field_mean: float32 [5], replicated
Inputs may be any that keep to these rules, and one draw needn't show every extreme that they name: `fields`: fields are positive cell means. For new node k of a pencil, node_cell lies cyclically between k - 14 and k + 13, and both ends are reached in every pencil; consecutive new nodes are at least 0.45 cells apart. `node_frac`: A multiple of 1/1024, below 1.
All inputs are finite; a program needn't handle non-finite values.
Results may differ from a plain program's by a relative error of at most 0.0003.
Values sent between devices are 32-bit elements; how exact they have to be, the bound alone decides.
A program may use at most 64 MiB of HBM per device.

v0:
```python
import jax
import jax.numpy as jnp
from jax import lax
from jax.sharding import PartitionSpec as P


def prefix(shard, axis, combine, identity):
    devices, mine = (lax.axis_size(axis), lax.axis_index(axis))
    everything = lax.all_gather(shard, axis)
    start = jnp.broadcast_to(jnp.asarray(identity, shard.dtype), shard.shape)

    def hop(k, before):
        reached = k < mine
        new = combine(before, everything[k])
        return jnp.where(reached, new, before)

    return lax.fori_loop(0, devices, hop, start)


def with_halo(block, sides, width):
    for axis, dim in sides:
        count = lax.axis_size(axis)
        forward = [(i, i + 1) for i in range(count - 1)]
        forward.append((count - 1, 0))
        backward = [(target, source) for source, target in forward]
        low = lax.ppermute(
            lax.slice_in_dim(block, block.shape[dim] - width, None, axis=dim), axis, forward
        )
        high = lax.ppermute(lax.slice_in_dim(block, 0, width, axis=dim), axis, backward)
        block = jnp.concatenate([low, block, high], axis=dim)
    return block


def from_behind(value, axis, steps):
    count = lax.axis_size(axis)
    pairs = [(source, (source + steps) % count) for source in range(count)]
    return lax.ppermute(value, axis, pairs)


def legendre_moments(padded):
    interior = padded.shape[-2] - 4
    left_cell = padded[..., 1 : interior + 2, :]
    right_cell = padded[..., 2 : interior + 3, :]
    faces = 7.0 / 12.0 * (left_cell + right_cell) - 1.0 / 12.0 * (
        padded[..., 0 : interior + 1, :] + padded[..., 3 : interior + 4, :]
    )
    faces = jnp.clip(faces, jnp.minimum(left_cell, right_cell), jnp.maximum(left_cell, right_cell))
    means = padded[..., 2 : interior + 2, :]
    face_low = faces[..., :interior, :]
    face_high = faces[..., 1:, :]
    is_flat = (face_high - means) * (means - face_low) <= 0.0
    face_low = jnp.where(is_flat, means, face_low)
    face_high = jnp.where(is_flat, means, face_high)
    jump_size = face_high - face_low
    centre = means - 0.5 * (face_low + face_high)
    threshold = jump_size * jump_size / 6.0
    low_final = jnp.where(jump_size * centre > threshold, 3.0 * means - 2.0 * face_high, face_low)
    high_final = jnp.where(-threshold > jump_size * centre, 3.0 * means - 2.0 * face_low, face_high)
    slopes = 0.5 * (high_final - low_final)
    curves = 0.5 * (low_final + high_final) - means
    return (slopes, curves)


def partial_mass(means, slopes, curves, fraction):
    return fraction * (
        means + slopes * (fraction - 1.0) + curves * ((2.0 * fraction - 3.0) * fraction + 1.0)
    )


def add_terms(first, second):
    return first + second


def select_window(stacked, lookup):
    indices = jnp.broadcast_to(lookup[None], (stacked.shape[0],) + lookup.shape)
    return jnp.take_along_axis(stacked, indices, axis=1)


def shards(fields, node_cell, node_frac):
    field_count, cell_count, pencils = fields.shape
    segments = lax.axis_size("gx")
    own_index = lax.axis_index("gx")
    length = cell_count * segments
    margin = cell_count - 2
    root = own_index * cell_count
    totals = jnp.sum(fields, axis=1)
    loop_mass = lax.psum(totals, "gx")
    offset = prefix(totals, "gx", add_terms, jnp.zeros_like(totals))
    padded = with_halo(fields, (("gx", 1),), 2)
    slopes, curves = legendre_moments(padded)
    mass_before = offset[:, None, :] + jnp.cumsum(fields, axis=1) - fields
    stacked = jnp.concatenate([mass_before, fields, slopes, curves], axis=0)
    extended = with_halo(stacked, (("gx", 1),), margin)
    before_wide = extended[0:field_count]
    means_wide = extended[field_count : 2 * field_count]
    slopes_wide = extended[2 * field_count : 3 * field_count]
    curves_wide = extended[3 * field_count : 4 * field_count]
    node_index = root + jnp.arange(cell_count, dtype=jnp.int32)[:, None]
    winding = (node_index - node_cell + length // 2) // length
    lookup = jnp.mod(node_cell - root + margin, length)
    quantities = jnp.concatenate([before_wide, means_wide, slopes_wide, curves_wide], axis=0)
    chosen = select_window(quantities, lookup)
    before_sel = chosen[0:field_count]
    means_sel = chosen[field_count : 2 * field_count]
    slopes_sel = chosen[2 * field_count : 3 * field_count]
    curves_sel = chosen[3 * field_count : 4 * field_count]
    mass_at = before_sel + partial_mass(means_sel, slopes_sel, curves_sel, node_frac[None])
    mass_at = mass_at + winding.astype(jnp.float32)[None] * loop_mass[:, None, :]
    anchor = node_cell + winding * length
    position = (anchor[:1] - root).astype(jnp.float32) + node_frac[:1]
    outgoing = jnp.concatenate([mass_at[:, :1], position[None]], axis=0)
    incoming = from_behind(outgoing, "gx", -1)
    closing = jnp.where(own_index == segments - 1, loop_mass, 0.0)
    after_first = incoming[:field_count, 0] + closing
    mass_after = jnp.concatenate([mass_at[:, 1:], after_first[:, None]], axis=1)
    masses = mass_after - mass_at
    interior = (anchor[1:] - anchor[:-1]).astype(jnp.float32) + node_frac[1:] - node_frac[:-1]
    final_width = (
        (root + cell_count - anchor[-1:]).astype(jnp.float32)
        + incoming[field_count]
        - node_frac[-1:]
    )
    widths = jnp.concatenate([interior, final_width], axis=0)
    remapped = masses / widths[None]
    field_sums = lax.psum(jnp.sum(masses, axis=(1, 2)), ("gx", "yz"))
    field_mean = field_sums / (length * pencils * lax.axis_size("yz"))
    return (remapped, field_mean)


def solution(mesh):
    in_specs = (P(None, "gx", "yz"), P("gx", "yz"), P("gx", "yz"))
    out_specs = (P(None, "gx", "yz"), P())
    return jax.shard_map(shards, mesh=mesh, in_specs=in_specs, out_specs=out_specs, check_vma=False)
```

profile of v0, /device:TPU:1, one launch (start us, length us, event | category | flops | bytes accessed | tf_op | source)
XLA Modules:
  0.0 909.6 jit_solution(2286665323723516787)
XLA Ops:
  0.6 0.0 copy-start
  0.6 0.0 copy-start.2
  0.7 0.8 fusion.31
  1.5 0.1 collective-permute-start.1
  1.6 2.6 collective-permute-start
  4.2 0.9 fusion.30
  5.1 21.2 %all-gather.1 = f32[16,5,256]{2,1,0:T(8,128)S(1)} all-gather(f32[1,5,256]{2,1,0:T(8,128)S(1)} %bitcast.20), channel_id=2, replica_groups=mesh['gx'=16,'yz'=2] {'gx'}, dimensions={0}, use_global_device_ids=true | all-gather | bytes 87040 | tf_op jit(solution)/shard_map/all_gather | solution.py:9
  26.3 0.5 while.14
  26.9 0.7 broadcast_compare_fusion
  27.6 0.0 copy-done.2
  27.7 0.1 fusion.22
  27.7 0.0 copy-done
  27.8 0.1 reduce_window_sum.11
  27.8 0.0 collective-permute-done.1
  27.9 0.0 collective-permute-done
  27.9 0.1 fusion.5
  28.0 0.1 subtract_multiply_fusion
  28.1 0.0 copy-start.1
  28.2 0.9 collective-permute-start.2
  29.1 0.0 collective-permute-start.3
  29.1 0.0 copy-done.1
  29.1 0.2 copy.8
  29.2 33.1 %psum.14 = f32[5,256]{1,0:T(8,128)S(1)} all-reduce(f32[5,256]{1,0:T(8,128)S(1)} %get-tuple-element.116), channel_id=1, replica_groups=mesh['gx'=16,'yz'=2] {'gx'}, use_global_device_ids=true, to_apply=%region_4.5 | all-reduce | flops 1280 | bytes 10240 | tf_op jit(solution)/shard_map/psum | solution.py:87
  62.3 0.0 collective-permute-done.2
  62.3 0.0 collective-permute-done.3
  62.4 0.1 pad_maximum_fusion
  62.5 804.2 %gather_fusion = f32[81920]{0:T(1024)S(1)} fusion(f32[20,44,256]{2,1,0:T(8,128)S(1)} %pad_maximum_fusion, s32[81920]{0:T(1024)S(1)} %bitcast.18), kind=kCustom, calls=%fused_computation | custom fusion | bytes 1638400 | tf_op jit(solution)/shard_map/jit(take_along_axis)/gather | solution.py:76
  866.7 0.1 reshape.34
  866.9 2.8 collective-permute-start.4
  869.8 0.8 collective-permute-done.4
  870.6 0.7 fusion.15
  871.3 37.8 %psum.15 = f32[5]{0:T(128)S(1)} all-reduce(f32[5]{0:T(128)S(1)} %get-tuple-element.113), channel_id=1, replica_groups=mesh['gx'=16,'yz'=2] {'gx','yz'}, use_global_device_ids=true, to_apply=%region_6.7 | all-reduce | flops 5 | bytes 40 | tf_op jit(solution)/shard_map/psum | solution.py:125
  909.1 0.5 broadcast_multiply_fusion
  (36 shorter events, 0.4 us)
Async XLA Ops:
  0.6 27.1 %copy-start = (f32[5,16,256]{2,1,0:T(8,128)S(1)}, f32[5,16,256]{2,1,0:T(8,128)}, u32[]{:S(2)}) copy-start(f32[5,16,256]{2,1,0:T(8,128)} %param.5) | copy-start | bytes 245764
  0.6 27.0 %copy-start.2 = (s32[16,256]{1,0:T(8,128)S(1)}, s32[16,256]{1,0:T(8,128)}, u32[]{:S(2)}) copy-start(s32[16,256]{1,0:T(8,128)} %param.6) | copy-start | bytes 49156
  1.5 26.3 %collective-permute-start.1 = (f32[5,2,256]{2,1,0:T(2,128)S(1)}, f32[5,2,256]{2,1,0:T(2,128)S(1)}, u32[]{:S(2)}, u32[]{:S(2)}) collective-permute-start(f32[5,2,256]{2,1,0:T(2,128)S(1)} %get-tuple-element.119), channel_id=1, source_target_pairs={{2,0},{4,2},{6,4},{8,6},{10,8},{12,10},{14,12},{16,14},{18,16},{20... | collective-permute-start | bytes 30728 | tf_op jit(solution)/shard_map/ppermute | solution.py:29
  1.6 26.3 %collective-permute-start = (f32[5,2,256]{2,1,0:T(2,128)S(1)}, f32[5,2,256]{2,1,0:T(2,128)S(1)}, u32[]{:S(2)}, u32[]{:S(2)}) collective-permute-start(f32[5,2,256]{2,1,0:T(2,128)S(1)} %get-tuple-element.118), channel_id=1, source_target_pairs={{0,2},{2,4},{4,6},{6,8},{8,10},{10,12},{12,14},{14,16},{16,18},{18... | collective-permute-start | bytes 30728 | tf_op jit(solution)/shard_map/ppermute | solution.py:26
  28.1 1.0 copy-start.1
  28.2 34.2 %collective-permute-start.2 = (f32[20,14,256]{2,1,0:T(8,128)S(1)}, f32[20,14,256]{2,1,0:T(8,128)S(1)}, u32[]{:S(2)}, u32[]{:S(2)}) collective-permute-start(f32[20,14,256]{2,1,0:T(8,128)S(1)} %get-tuple-element.109), channel_id=1, source_target_pairs={{0,2},{2,4},{4,6},{6,8},{8,10},{10,12},{12,14},{14,16},{16,18},{18... | collective-permute-start | bytes 860168 | tf_op jit(solution)/shard_map/ppermute | solution.py:26
  29.1 33.3 %collective-permute-start.3 = (f32[20,14,256]{2,1,0:T(8,128)S(1)}, f32[20,14,256]{2,1,0:T(8,128)S(1)}, u32[]{:S(2)}, u32[]{:S(2)}) collective-permute-start(f32[20,14,256]{2,1,0:T(8,128)S(1)} %get-tuple-element.110), channel_id=1, source_target_pairs={{2,0},{4,2},{6,4},{8,6},{10,8},{12,10},{14,12},{16,14},{18,16},{20... | collective-permute-start | bytes 860168 | tf_op jit(solution)/shard_map/ppermute | solution.py:29
  866.9 3.6 collective-permute-start.4
where the time goes:
time: 911 us; the launch traced here: 910 us
  local copies, waits for them, and re-layouts  805 us (88%)
  blocking collectives  92 us (10%)
    gather x2, local copies, waits for them, and re-layouts, select_window(): return jnp.take_along_axis(stacked, indices, axis=1)  804 us
    psum x1, blocking collectives, shards(): field_sums = lax.psum(jnp.sum(masses, axis=(1, 2)), ('gx', 'yz'))  37.8 us
    psum x1, blocking collectives, shards(): loop_mass = lax.psum(totals, 'gx')  33.1 us
    all_gather x1, blocking collectives, prefix(): everything = lax.all_gather(shard, axis)  21.2 us
  transfers between devices with their start and end apart: 5, of which 1 were waited for; matrix products, arithmetic and copies ran while one was open for 0% of the time, Pallas kernels for 0%

commit v1 on v0

v1 whole, which is shorter than its diff:
```python
import functools

import jax
import jax.numpy as jnp
from jax import lax
from jax.experimental import pallas as pl
from jax.experimental.pallas import tpu as pltpu
from jax.sharding import PartitionSpec as P

MESH = pl.DeviceIdType.MESH
LANES = 128
SUB = 8


def legendre_moments(means):
    rows = means.shape[0]
    right = pltpu.roll(means, rows - 1, 0)
    outer = pltpu.roll(means, 1, 0) + pltpu.roll(means, rows - 2, 0)
    faces = 7.0 / 12.0 * (means + right) - 1.0 / 12.0 * outer
    faces = jnp.clip(faces, jnp.minimum(means, right), jnp.maximum(means, right))
    face_low = pltpu.roll(faces, 1, 0)
    face_high = faces
    is_flat = (face_high - means) * (means - face_low) <= 0.0
    face_low = jnp.where(is_flat, means, face_low)
    face_high = jnp.where(is_flat, means, face_high)
    jump_size = face_high - face_low
    centre = means - 0.5 * (face_low + face_high)
    threshold = jump_size * jump_size * (1.0 / 6.0)
    tilt = jump_size * centre
    low_final = jnp.where(tilt > threshold, 3.0 * means - 2.0 * face_high, face_low)
    high_final = jnp.where(-threshold > tilt, 3.0 * means - 2.0 * face_low, face_high)
    slopes = 0.5 * (high_final - low_final)
    curves = 0.5 * (low_final + high_final) - means
    return slopes, curves


def pick(table, index):
    return jnp.take_along_axis(table, index, axis=0, mode="promise_in_bounds")


def kernel(
    sizes, fields_ref, cell_ref, frac_ref, out_ref, mean_ref,
    ext, nodes, fracs, slots, local_sem, send_sem, recv_sem, msg_send, msg_recv,
):
    segments, slabs, field_count, cells, pencils = sizes
    total = segments * slabs
    length = segments * cells
    margin = cells - 2
    own = lax.axis_index("gx")
    slab = lax.axis_index("yz")
    me = own * slabs + slab
    root = own * cells

    def peer(step):
        flat = lax.rem(me + step, total)
        return {"gx": flat // slabs, "yz": lax.rem(flat, slabs)}

    load_fields = pltpu.make_async_copy(fields_ref, ext.at[:, pl.ds(cells, cells)], local_sem.at[0])
    load_cell = pltpu.make_async_copy(cell_ref, nodes.at[pl.ds(0, cells)], local_sem.at[1])
    load_frac = pltpu.make_async_copy(frac_ref, fracs.at[pl.ds(0, cells)], local_sem.at[2])
    load_fields.start()
    load_cell.start()
    load_frac.start()

    barrier = pltpu.get_barrier_semaphore()

    def greet(step, carry):
        pl.semaphore_signal(barrier, inc=1, device_id=peer(step), device_id_type=MESH)
        return carry

    lax.fori_loop(1, total, greet, 0)

    load_fields.wait()
    lane = lax.broadcasted_iota(jnp.int32, (1, LANES), 1)
    message = jnp.zeros((1, LANES), jnp.float32)
    for f in range(field_count):
        part = jnp.sum(ext[f, cells : 2 * cells, :], keepdims=True)
        message = jnp.where(lane == f, part, message)
    slots[0] = message
    load_cell.wait()
    load_frac.wait()
    pl.semaphore_wait(barrier, total - 1)

    right = {"gx": lax.rem(own + 1, segments)}
    left = {"gx": lax.rem(own + segments - 1, segments)}
    block = ext.at[:, pl.ds(cells, cells)]
    copies = [
        (nodes.at[pl.ds(0, SUB)], nodes.at[pl.ds(cells, SUB)], left),
        (fracs.at[pl.ds(0, SUB)], fracs.at[pl.ds(cells, SUB)], left),
        (block, ext.at[:, pl.ds(2 * cells, cells)], left),
        (block, ext.at[:, pl.ds(0, cells)], right),
    ]
    copies = [
        pltpu.make_async_remote_copy(
            src_ref=source, dst_ref=target, send_sem=send_sem.at[i], recv_sem=recv_sem.at[i],
            device_id=who, device_id_type=MESH,
        )
        for i, (source, target, who) in enumerate(copies)
    ]
    for copy in copies:
        copy.start()

    def send(step, carry):
        pltpu.make_async_remote_copy(
            src_ref=slots.at[0], dst_ref=slots.at[step], send_sem=msg_send, recv_sem=msg_recv,
            device_id=peer(step), device_id_type=MESH,
        ).start()
        return carry

    lax.fori_loop(1, total, send, 0)
    for copy in copies:
        copy.wait_recv()

    node_rows = cells + SUB
    node_index = root + lax.broadcasted_iota(jnp.int32, (node_rows, LANES), 0)
    row_id = lax.broadcasted_iota(jnp.int32, (cells, LANES), 0)
    groups = 3 * cells // SUB
    origin = cells // SUB
    low_row = cells - margin
    high_row = cells + margin - 1
    sub_id = lax.broadcasted_iota(jnp.int32, (groups, SUB, LANES), 1)

    for half in range(pencils // LANES):
        span = slice(half * LANES, (half + 1) * LANES)
        cell = nodes[:, span]
        frac = fracs[:, span]
        shifted = node_index - cell + length // 2
        cell = jnp.where(shifted < 0, cell - length, jnp.where(shifted >= length, cell + length, cell))
        place = cell - root + cells
        group = place // SUB
        index = place % SUB
        position = place.astype(jnp.float32)
        after_cell = jnp.concatenate([position[1:cells], position[cells : cells + 1]], axis=0)
        after_frac = jnp.concatenate([frac[1:cells], frac[cells : cells + 1]], axis=0)
        inverse = 1.0 / ((after_cell - position[:cells]) + after_frac - frac[:cells])

        for f in range(field_count):
            means = ext[f, :, span]
            slopes, curves = legendre_moments(means)
            stack = means.reshape(groups, SUB, LANES)
            running = stack
            for step in (1, 2, 4):
                running = running + jnp.where(sub_id >= step, pltpu.roll(running, step, 1), 0.0)
            before = running - stack
            bases = [None] * groups
            bases[origin] = jnp.zeros((1, LANES), jnp.float32)
            for g in range(origin + 1, groups):
                bases[g] = bases[g - 1] + running[g - 1, SUB - 1 : SUB]
            for g in range(origin - 1, -1, -1):
                bases[g] = bases[g + 1] - running[g, SUB - 1 : SUB]
            tables = []
            for g in range(groups):
                at = slice(g * SUB, (g + 1) * SUB)
                tables.append((before[g] + bases[g], stack[g], slopes[at], curves[at]))

            blocks = []
            for b in range(cells // SUB + 1):
                at = slice(b * SUB, (b + 1) * SUB)
                first = (b * SUB + low_row) // SUB
                last_node = b * SUB + SUB - 1 if b < cells // SUB else b * SUB
                last = (last_node + high_row) // SUB
                chosen = [None] * 4
                for g in range(first, last + 1):
                    for i in range(4):
                        got = pick(tables[g][i], index[at])
                        chosen[i] = got if chosen[i] is None else jnp.where(group[at] == g, got, chosen[i])
                t = frac[at]
                base, mean, slope, curve = chosen
                blocks.append(
                    base + t * (mean + slope * (t - 1.0) + curve * ((2.0 * t - 3.0) * t + 1.0))
                )
            mass = jnp.concatenate(blocks[:-1], axis=0)
            after = jnp.where(row_id == cells - 1, blocks[-1][0:1], pltpu.roll(mass, cells - 1, 0))
            out_ref[f, :, span] = (after - mass) * inverse

    arrived = pltpu.make_async_copy(
        slots.at[pl.ds(1, total - 1)], slots.at[pl.ds(1, total - 1)], msg_recv
    )
    arrived.wait()
    summed = jnp.sum(slots[...], axis=0) * (1.0 / (length * pencils * slabs))
    mean_ref[...] = summed
    for copy in copies:
        copy.wait_send()
    pltpu.make_async_copy(
        slots.at[pl.ds(1, total - 1)], slots.at[pl.ds(1, total - 1)], msg_send
    ).wait()


def shards(fields, node_cell, node_frac):
    field_count, cells, pencils = fields.shape
    segments = lax.axis_size("gx")
    slabs = lax.axis_size("yz")
    total = segments * slabs
    sizes = (segments, slabs, field_count, cells, pencils)
    dma = pltpu.SemaphoreType.DMA
    remapped, mean = pl.pallas_call(
        functools.partial(kernel, sizes),
        out_shape=(
            jax.ShapeDtypeStruct(fields.shape, jnp.float32),
            jax.ShapeDtypeStruct((1, LANES), jnp.float32),
        ),
        in_specs=[pl.BlockSpec(memory_space=pl.ANY)] * 3,
        out_specs=(
            pl.BlockSpec(memory_space=pltpu.VMEM),
            pl.BlockSpec(memory_space=pltpu.VMEM),
        ),
        scratch_shapes=[
            pltpu.VMEM((field_count, 3 * cells, pencils), jnp.float32),
            pltpu.VMEM((cells + SUB, pencils), jnp.int32),
            pltpu.VMEM((cells + SUB, pencils), jnp.float32),
            pltpu.VMEM((total, 1, LANES), jnp.float32),
            dma((3,)),
            dma((4,)),
            dma((4,)),
            dma,
            dma,
        ],
        compiler_params=pltpu.CompilerParams(collective_id=0, has_side_effects=True),
    )(fields, node_cell, node_frac)
    return remapped, mean[0, :field_count]


def solution(mesh):
    in_specs = (P(None, "gx", "yz"), P("gx", "yz"), P("gx", "yz"))
    out_specs = (P(None, "gx", "yz"), P())
    return jax.shard_map(shards, mesh=mesh, in_specs=in_specs, out_specs=out_specs, check_vma=False)
```

time: 911 us -> 15.5 us (0.02)
  local copies, waits for them, and re-layouts: 805 us -> 2.71 us
  blocking collectives: 92 us -> 0 us
  Pallas kernels: 0 us -> 12 us
    gather x2 -> x0, local copies, waits for them, and re-layouts: 804 us -> none  [select_window(): return jnp.take_along_axis(stacked, indices, axis=1)]
    psum x2 -> x0, blocking collectives: 70.8 us -> none  [the longest x1 37.8 us: shards(): field_sums = lax.psum(jnp.sum(masses, axis=(1, 2)), ('gx', 'yz'))]
    all_gather x1 -> x0, blocking collectives: 21.2 us -> none  [prefix(): everything = lax.all_gather(shard, axis)]
    pallas_call x0 -> x1, Pallas kernels: none -> 12 us  [shards(): pl.pallas_call(functools.partial(kernel, sizes), out_shape=(jax.ShapeDtyp...]
  transfers between devices with their start and end apart: 5 -> 0, of which waited for: 1 -> 0; matrix products, arithmetic and copies ran while one was open for 0% -> 0% of each run, Pallas kernels for 0% -> 0%
where the time goes in v1:
time: 15.5 us; the launch traced here: 15.3 us
  Pallas kernels  12 us (77%)
  local copies, waits for them, and re-layouts  2.71 us (17%)
  between operations  0.65 us (4%)
    pallas_call x1, Pallas kernels, shards(): pl.pallas_call(functools.partial(kernel, sizes), out_shape=(jax.ShapeDtyp...  12 us
    unnamed x3, local copies, waits for them, and re-layouts  2.2 us
    squeeze x1, local copies, waits for them, and re-layouts, shards(): return (remapped, mean[0, :field_count])  0.51 us

profile of v1, /device:TPU:1, one launch (start us, length us, event | category | flops | bytes accessed | tf_op | source)
XLA Modules:
  0.0 15.3 jit_solution(3920147979482968178)
XLA Ops:
  0.6 12.0 %shard_map.50 = (f32[5,16,256]{2,1,0:T(8,128)}, f32[1,128]{1,0:T(1,128)}) custom-call(f32[5,16,256]{2,1,0:T(8,128)} %fields_ref.1, s32[16,256]{1,0:T(8,128)} %cell_ref.1, f32[16,256]{1,0:T(8,128)} %frac_ref.1), custom_call_target="tpu_custom_call" | custom-call | tf_op jit(solution)/shard_map/pallas_call | solution.py:196
  12.6 0.0 copy-start
  12.6 0.7 %copy-done = f32[1,128]{1,0:T(1,128)S(1)} copy-done((f32[1,128]{1,0:T(1,128)S(1)}, f32[1,128]{1,0:T(1,128)}, u32[]{:S(2)}) %copy-start) | copy-done | bytes 536
  13.3 0.5 %slice_bitcast_fusion = f32[5]{0:T(128)} fusion(f32[1,128]{1,0:T(1,128)S(1)} %copy-done), kind=kLoop, calls=%fused_computation | loop fusion | bytes 40 | tf_op jit(solution)/shard_map/squeeze | solution.py:220
  13.8 1.5 %copy.6 = f32[5,16,256]{2,1,0:T(8,128)} copy(f32[5,16,256]{2,1,0:T(8,128)} %get-tuple-element.8) | data formatting | bytes 163840
Async XLA Ops:
  12.6 0.7 %copy-start = (f32[1,128]{1,0:T(1,128)S(1)}, f32[1,128]{1,0:T(1,128)}, u32[]{:S(2)}) copy-start(f32[1,128]{1,0:T(1,128)} %get-tuple-element.5) | copy-start | bytes 1540

commit v2 on v1

--- a/solution.py
+++ b/solution.py
@@ -178,12 +178,21 @@
     )
     arrived.wait()
     summed = jnp.sum(slots[...], axis=0) * (1.0 / (length * pencils * slabs))
-    mean_ref[...] = summed
+    mean_ref[...] = summed[0, :field_count]
     for copy in copies:
         copy.wait_send()
     pltpu.make_async_copy(
         slots.at[pl.ds(1, total - 1)], slots.at[pl.ds(1, total - 1)], msg_send
     ).wait()
+
+
+def put(new_ref, mean_ref, new_out, mean_out, sem):
+    new_copy = pltpu.make_async_copy(new_ref, new_out, sem.at[0])
+    mean_copy = pltpu.make_async_copy(mean_ref, mean_out, sem.at[1])
+    new_copy.start()
+    mean_copy.start()
+    new_copy.wait()
+    mean_copy.wait()
 
 
 def shards(fields, node_cell, node_frac):
@@ -196,8 +205,8 @@
     remapped, mean = pl.pallas_call(
         functools.partial(kernel, sizes),
         out_shape=(
-            jax.ShapeDtypeStruct(fields.shape, jnp.float32),
-            jax.ShapeDtypeStruct((1, LANES), jnp.float32),
+            pltpu.VMEM(fields.shape, jnp.float32),
+            pltpu.VMEM((field_count,), jnp.float32),
         ),
         in_specs=[pl.BlockSpec(memory_space=pl.ANY)] * 3,
         out_specs=(
@@ -217,7 +226,19 @@
         ],
         compiler_params=pltpu.CompilerParams(collective_id=0, has_side_effects=True),
     )(fields, node_cell, node_frac)
-    return remapped, mean[0, :field_count]
+    return pl.pallas_call(
+        put,
+        out_shape=(
+            jax.ShapeDtypeStruct(fields.shape, jnp.float32),
+            jax.ShapeDtypeStruct((field_count,), jnp.float32),
+        ),
+        in_specs=[pl.BlockSpec(memory_space=pltpu.VMEM)] * 2,
+        out_specs=(pl.BlockSpec(memory_space=pl.ANY),) * 2,
+        scratch_shapes=[dma((2,))],
+    )(
+        pltpu.with_memory_space_constraint(remapped, pltpu.VMEM),
+        pltpu.with_memory_space_constraint(mean, pltpu.VMEM),
+    )
 
 
 def solution(mesh):

time: 15.5 us -> 12.8 us (0.83)
  local copies, waits for them, and re-layouts: 2.71 us -> 0 us
    unnamed x3 -> x0, local copies, waits for them, and re-layouts: 2.2 us -> none
    squeeze x1 -> x0, local copies, waits for them, and re-layouts: 0.51 us -> none  [shards(): return (remapped, mean[0, :field_count])]
    pallas_call x1 -> x2, Pallas kernels: 12 us -> 12 us  [the longest x1 11.3 us: shards(): pl.pallas_call(functools.partial(kernel, sizes), out_shape=(pltpu.VMEM(fi...]
where the time goes in v2:
time: 12.8 us; the launch traced here: 12.6 us
  Pallas kernels  12 us (94%)
  between operations  0.64 us (5%)
    pallas_call x1, Pallas kernels, shards(): pl.pallas_call(functools.partial(kernel, sizes), out_shape=(pltpu.VMEM(fi...  11.3 us
    pallas_call x1, Pallas kernels, shards(): pl.pallas_call(put, out_shape=(jax.ShapeDtypeStruct(fields.shape, jnp.flo...  0.66 us

profile of v2, /device:TPU:1, one launch (start us, length us, event | category | flops | bytes accessed | tf_op | source)
XLA Modules:
  0.0 12.6 jit_solution(1726376156546982003)
XLA Ops:
  0.6 11.3 %shard_map.50 = (f32[5,16,256]{2,1,0:T(8,128)S(1)}, f32[5]{0:T(128)S(1)}) custom-call(f32[5,16,256]{2,1,0:T(8,128)} %fields_ref.1, s32[16,256]{1,0:T(8,128)} %cell_ref.1, f32[16,256]{1,0:T(8,128)} %frac_ref.1), custom_call_target="tpu_custom_call" | custom-call | tf_op jit(solution)/shard_map/pallas_call | solution.py:205
  12.0 0.7 %shard_map.51 = (f32[5,16,256]{2,1,0:T(8,128)}, f32[5]{0:T(128)}) custom-call(f32[5,16,256]{2,1,0:T(8,128)S(1)} %get-tuple-element.4.new_ref, f32[5]{0:T(128)S(1)} %get-tuple-element.5.mean_ref), custom_call_target="tpu_custom_call" | custom-call | tf_op jit(solution)/shard_map/pallas_call | solution.py:229

commit v3 on v2

--- a/solution.py
+++ b/solution.py
@@ -40,20 +40,29 @@
 
 def kernel(
     sizes, fields_ref, cell_ref, frac_ref, out_ref, mean_ref,
-    ext, nodes, fracs, slots, local_sem, send_sem, recv_sem, msg_send, msg_recv,
+    ext, nodes, fracs, slots, far_slots, local_sem, send_sem, recv_sem, msg_send, msg_recv,
 ):
-    segments, slabs, field_count, cells, pencils = sizes
-    total = segments * slabs
+    segments, slabs, blocks, field_count, cells, pencils = sizes
     length = segments * cells
     margin = cells - 2
     own = lax.axis_index("gx")
     slab = lax.axis_index("yz")
-    me = own * slabs + slab
     root = own * cells
 
-    def peer(step):
-        flat = lax.rem(me + step, total)
-        return {"gx": flat // slabs, "yz": lax.rem(flat, slabs)}
+    width = segments // blocks
+    near = width * slabs
+    here = lax.rem(own, width) * slabs + slab
+    block_id = own // width
+
+    def near_peer(step):
+        flat = lax.rem(here + step, near)
+        return {"gx": block_id * width + flat // slabs, "yz": lax.rem(flat, slabs)}
+
+    def far_peer(step):
+        return {"gx": lax.rem(block_id + step, blocks) * width + lax.rem(own, width)}
+
+    right = {"gx": lax.rem(own + 1, segments)}
+    left = {"gx": lax.rem(own + segments - 1, segments)}
 
     load_fields = pltpu.make_async_copy(fields_ref, ext.at[:, pl.ds(cells, cells)], local_sem.at[0])
     load_cell = pltpu.make_async_copy(cell_ref, nodes.at[pl.ds(0, cells)], local_sem.at[1])
@@ -64,11 +73,17 @@
 
     barrier = pltpu.get_barrier_semaphore()
 
-    def greet(step, carry):
-        pl.semaphore_signal(barrier, inc=1, device_id=peer(step), device_id_type=MESH)
-        return carry
-
-    lax.fori_loop(1, total, greet, 0)
+    def greet(who):
+        pl.semaphore_signal(barrier, inc=1, device_id=who, device_id_type=MESH)
+
+    greet(right)
+    greet(left)
+    for step in range(1, blocks):
+        greet(far_peer(step))
+
+    @pl.loop(1, near)
+    def _(step):
+        greet(near_peer(step))
 
     load_fields.wait()
     lane = lax.broadcasted_iota(jnp.int32, (1, LANES), 1)
@@ -79,37 +94,79 @@
     slots[0] = message
     load_cell.wait()
     load_frac.wait()
-    pl.semaphore_wait(barrier, total - 1)
-
-    right = {"gx": lax.rem(own + 1, segments)}
-    left = {"gx": lax.rem(own + segments - 1, segments)}
+    pl.semaphore_wait(barrier, near + blocks)
+
     block = ext.at[:, pl.ds(cells, cells)]
-    copies = [
-        (nodes.at[pl.ds(0, SUB)], nodes.at[pl.ds(cells, SUB)], left),
-        (fracs.at[pl.ds(0, SUB)], fracs.at[pl.ds(cells, SUB)], left),
-        (block, ext.at[:, pl.ds(2 * cells, cells)], left),
-        (block, ext.at[:, pl.ds(0, cells)], right),
-    ]
-    copies = [
-        pltpu.make_async_remote_copy(
+
+    def push(i, source, target, who):
+        return pltpu.make_async_remote_copy(
             src_ref=source, dst_ref=target, send_sem=send_sem.at[i], recv_sem=recv_sem.at[i],
             device_id=who, device_id_type=MESH,
         )
-        for i, (source, target, who) in enumerate(copies)
+
+    to_left = push(0, block, ext.at[:, pl.ds(2 * cells, cells)], left)
+    to_right = push(1, block, ext.at[:, pl.ds(0, cells)], right)
+    first_cell = push(2, nodes.at[pl.ds(0, SUB)], nodes.at[pl.ds(cells, SUB)], left)
+    first_frac = push(3, fracs.at[pl.ds(0, SUB)], fracs.at[pl.ds(cells, SUB)], left)
+    copies = [to_left, to_right, first_cell, first_frac]
+
+    yield_right = own == 1
+    yield_left = own == segments - 2
+
+    @pl.when(jnp.logical_not(yield_right))
+    def _():
+        to_right.start()
+
+    @pl.when(jnp.logical_not(yield_left))
+    def _():
+        to_left.start()
+
+    @pl.loop(1, near)
+    def _(step):
+        pltpu.make_async_remote_copy(
+            src_ref=slots.at[0], dst_ref=slots.at[step], send_sem=msg_send.at[0],
+            recv_sem=msg_recv.at[0], device_id=near_peer(step), device_id_type=MESH,
+        ).start()
+
+    first_cell.start()
+    first_frac.start()
+
+    @pl.when(yield_right)
+    def _():
+        to_right.wait_recv()
+        to_right.start()
+
+    @pl.when(yield_left)
+    def _():
+        to_left.wait_recv()
+        to_left.start()
+
+    def all_slots(ref, count, sem):
+        part = ref.at[pl.ds(1, count - 1)]
+        return pltpu.make_async_copy(part, part, sem)
+
+    all_slots(slots, near, msg_recv.at[0]).wait()
+    far_slots[0] = jnp.sum(slots[...], axis=0)
+    far_copies = [
+        pltpu.make_async_remote_copy(
+            src_ref=far_slots.at[0], dst_ref=far_slots.at[step], send_sem=msg_send.at[1],
+            recv_sem=msg_recv.at[1], device_id=far_peer(step), device_id_type=MESH,
+        )
+        for step in range(1, blocks)
     ]
-    for copy in copies:
+    for copy in far_copies:
         copy.start()
 
-    def send(step, carry):
-        pltpu.make_async_remote_copy(
-            src_ref=slots.at[0], dst_ref=slots.at[step], send_sem=msg_send, recv_sem=msg_recv,
-            device_id=peer(step), device_id_type=MESH,
-        ).start()
-        return carry
-
-    lax.fori_loop(1, total, send, 0)
-    for copy in copies:
-        copy.wait_recv()
+    first_cell.wait_recv()
+    first_frac.wait_recv()
+
+    @pl.when(jnp.logical_not(yield_right))
+    def _():
+        to_right.wait_recv()
+
+    @pl.when(jnp.logical_not(yield_left))
+    def _():
+        to_left.wait_recv()
 
     node_rows = cells + SUB
     node_index = root + lax.broadcasted_iota(jnp.int32, (node_rows, LANES), 0)
@@ -153,7 +210,7 @@
                 at = slice(g * SUB, (g + 1) * SUB)
                 tables.append((before[g] + bases[g], stack[g], slopes[at], curves[at]))
 
-            blocks = []
+            parts = []
             for b in range(cells // SUB + 1):
                 at = slice(b * SUB, (b + 1) * SUB)
                 first = (b * SUB + low_row) // SUB
@@ -166,24 +223,20 @@
                         chosen[i] = got if chosen[i] is None else jnp.where(group[at] == g, got, chosen[i])
                 t = frac[at]
                 base, mean, slope, curve = chosen
-                blocks.append(
+                parts.append(
                     base + t * (mean + slope * (t - 1.0) + curve * ((2.0 * t - 3.0) * t + 1.0))
                 )
-            mass = jnp.concatenate(blocks[:-1], axis=0)
-            after = jnp.where(row_id == cells - 1, blocks[-1][0:1], pltpu.roll(mass, cells - 1, 0))
+            mass = jnp.concatenate(parts[:-1], axis=0)
+            after = jnp.where(row_id == cells - 1, parts[-1][0:1], pltpu.roll(mass, cells - 1, 0))
             out_ref[f, :, span] = (after - mass) * inverse
 
-    arrived = pltpu.make_async_copy(
-        slots.at[pl.ds(1, total - 1)], slots.at[pl.ds(1, total - 1)], msg_recv
-    )
-    arrived.wait()
-    summed = jnp.sum(slots[...], axis=0) * (1.0 / (length * pencils * slabs))
+    all_slots(far_slots, blocks, msg_recv.at[1]).wait()
+    summed = jnp.sum(far_slots[...], axis=0) * (1.0 / (length * pencils * slabs))
     mean_ref[...] = summed[0, :field_count]
     for copy in copies:
         copy.wait_send()
-    pltpu.make_async_copy(
-        slots.at[pl.ds(1, total - 1)], slots.at[pl.ds(1, total - 1)], msg_send
-    ).wait()
+    all_slots(slots, near, msg_send.at[0]).wait()
+    all_slots(far_slots, blocks, msg_send.at[1]).wait()
 
 
 def put(new_ref, mean_ref, new_out, mean_out, sem):
@@ -199,8 +252,8 @@
     field_count, cells, pencils = fields.shape
     segments = lax.axis_size("gx")
     slabs = lax.axis_size("yz")
-    total = segments * slabs
-    sizes = (segments, slabs, field_count, cells, pencils)
+    blocks = next(n for n in (4, 2) if segments % n == 0)
+    sizes = (segments, slabs, blocks, field_count, cells, pencils)
     dma = pltpu.SemaphoreType.DMA
     remapped, mean = pl.pallas_call(
         functools.partial(kernel, sizes),
@@ -217,12 +270,13 @@
             pltpu.VMEM((field_count, 3 * cells, pencils), jnp.float32),
             pltpu.VMEM((cells + SUB, pencils), jnp.int32),
             pltpu.VMEM((cells + SUB, pencils), jnp.float32),
-            pltpu.VMEM((total, 1, LANES), jnp.float32),
+            pltpu.VMEM((segments // blocks * slabs, 1, LANES), jnp.float32),
+            pltpu.VMEM((blocks, 1, LANES), jnp.float32),
             dma((3,)),
             dma((4,)),
             dma((4,)),
-            dma,
-            dma,
+            dma((2,)),
+            dma((2,)),
         ],
         compiler_params=pltpu.CompilerParams(collective_id=0, has_side_effects=True),
     )(fields, node_cell, node_frac)

time: 12.8 us -> 14.4 us (1.12)
  the two profiles are of different devices: /device:TPU:1 before, /device:TPU:0 now
where the time goes in v3:
time: 14.4 us; the launch traced here: 14.2 us
  Pallas kernels  13.6 us (94%)
  between operations  0.64 us (4%)
    pallas_call x1, Pallas kernels, shards(): pl.pallas_call(functools.partial(kernel, sizes), out_shape=(pltpu.VMEM(fi...  12.9 us
    pallas_call x1, Pallas kernels, shards(): pl.pallas_call(put, out_shape=(jax.ShapeDtypeStruct(fields.shape, jnp.flo...  0.66 us

profile of v3, /device:TPU:0, one launch (start us, length us, event | category | flops | bytes accessed | tf_op | source)
XLA Modules:
  0.0 14.2 jit_solution(13091427736697836626)
XLA Ops:
  0.6 12.9 %shard_map.50 = (f32[5,16,256]{2,1,0:T(8,128)S(1)}, f32[5]{0:T(128)S(1)}) custom-call(f32[5,16,256]{2,1,0:T(8,128)} %fields_ref.1, s32[16,256]{1,0:T(8,128)} %cell_ref.1, f32[16,256]{1,0:T(8,128)} %frac_ref.1), custom_call_target="tpu_custom_call" | custom-call | tf_op jit(solution)/shard_map/pallas_call | solution.py:258
  13.6 0.7 %shard_map.51 = (f32[5,16,256]{2,1,0:T(8,128)}, f32[5]{0:T(128)}) custom-call(f32[5,16,256]{2,1,0:T(8,128)S(1)} %get-tuple-element.4.new_ref, f32[5]{0:T(128)S(1)} %get-tuple-element.5.mean_ref), custom_call_target="tpu_custom_call" | custom-call | tf_op jit(solution)/shard_map/pallas_call | solution.py:283

commit v4 on v2

--- a/solution.py
+++ b/solution.py
@@ -48,12 +48,20 @@
     margin = cells - 2
     own = lax.axis_index("gx")
     slab = lax.axis_index("yz")
-    me = own * slabs + slab
     root = own * cells
 
-    def peer(step):
-        flat = lax.rem(me + step, total)
-        return {"gx": flat // slabs, "yz": lax.rem(flat, slabs)}
+    def wrap(value, size):
+        return jnp.where(value >= size, value - size, value)
+
+    def others(visit):
+        for dy in range(1, slabs):
+            visit(dy, {"yz": wrap(slab + dy, slabs)})
+
+        @pl.loop(1, segments)
+        def _(dx):
+            gx = wrap(own + dx, segments)
+            for dy in range(slabs):
+                visit(dx * slabs + dy, {"gx": gx, "yz": wrap(slab + dy, slabs)})
 
     load_fields = pltpu.make_async_copy(fields_ref, ext.at[:, pl.ds(cells, cells)], local_sem.at[0])
     load_cell = pltpu.make_async_copy(cell_ref, nodes.at[pl.ds(0, cells)], local_sem.at[1])
@@ -64,12 +72,10 @@
 
     barrier = pltpu.get_barrier_semaphore()
 
-    def greet(step, carry):
-        pl.semaphore_signal(barrier, inc=1, device_id=peer(step), device_id_type=MESH)
-        return carry
-
-    lax.fori_loop(1, total, greet, 0)
-
+    def greet(slot, who):
+        pl.semaphore_signal(barrier, inc=1, device_id=who, device_id_type=MESH)
+
+    others(greet)
     load_fields.wait()
     lane = lax.broadcasted_iota(jnp.int32, (1, LANES), 1)
     message = jnp.zeros((1, LANES), jnp.float32)
@@ -81,15 +87,16 @@
     load_frac.wait()
     pl.semaphore_wait(barrier, total - 1)
 
-    right = {"gx": lax.rem(own + 1, segments)}
-    left = {"gx": lax.rem(own + segments - 1, segments)}
-    block = ext.at[:, pl.ds(cells, cells)]
+    right = {"gx": wrap(own + 1, segments)}
+    left = {"gx": wrap(own + segments - 1, segments)}
     copies = [
         (nodes.at[pl.ds(0, SUB)], nodes.at[pl.ds(cells, SUB)], left),
         (fracs.at[pl.ds(0, SUB)], fracs.at[pl.ds(cells, SUB)], left),
-        (block, ext.at[:, pl.ds(2 * cells, cells)], left),
-        (block, ext.at[:, pl.ds(0, cells)], right),
     ]
+    for f in range(field_count):
+        block = ext.at[f, pl.ds(cells, cells)]
+        copies.append((block, ext.at[f, pl.ds(2 * cells, cells)], left))
+        copies.append((block, ext.at[f, pl.ds(0, cells)], right))
     copies = [
         pltpu.make_async_remote_copy(
             src_ref=source, dst_ref=target, send_sem=send_sem.at[i], recv_sem=recv_sem.at[i],
@@ -97,18 +104,16 @@
         )
         for i, (source, target, who) in enumerate(copies)
     ]
+    def send(slot, who):
+        pltpu.make_async_remote_copy(
+            src_ref=slots.at[0], dst_ref=slots.at[slot], send_sem=msg_send, recv_sem=msg_recv,
+            device_id=who, device_id_type=MESH,
+        ).start()
+
+    others(send)
     for copy in copies:
         copy.start()
-
-    def send(step, carry):
-        pltpu.make_async_remote_copy(
-            src_ref=slots.at[0], dst_ref=slots.at[step], send_sem=msg_send, recv_sem=msg_recv,
-            device_id=peer(step), device_id_type=MESH,
-        ).start()
-        return carry
-
-    lax.fori_loop(1, total, send, 0)
-    for copy in copies:
+    for copy in copies[:2]:
         copy.wait_recv()
 
     node_rows = cells + SUB
@@ -120,6 +125,7 @@
     high_row = cells + margin - 1
     sub_id = lax.broadcasted_iota(jnp.int32, (groups, SUB, LANES), 1)
 
+    halves = []
     for half in range(pencils // LANES):
         span = slice(half * LANES, (half + 1) * LANES)
         cell = nodes[:, span]
@@ -134,7 +140,12 @@
         after_frac = jnp.concatenate([frac[1:cells], frac[cells : cells + 1]], axis=0)
         inverse = 1.0 / ((after_cell - position[:cells]) + after_frac - frac[:cells])
 
-        for f in range(field_count):
+        halves.append((span, frac, group, index, inverse))
+
+    for f in range(field_count):
+        for copy in copies[2 + 2 * f : 4 + 2 * f]:
+            copy.wait_recv()
+        for span, frac, group, index, inverse in halves:
             means = ext[f, :, span]
             slopes, curves = legendre_moments(means)
             stack = means.reshape(groups, SUB, LANES)
@@ -219,8 +230,8 @@
             pltpu.VMEM((cells + SUB, pencils), jnp.float32),
             pltpu.VMEM((total, 1, LANES), jnp.float32),
             dma((3,)),
-            dma((4,)),
-            dma((4,)),
+            dma((2 + 2 * field_count,)),
+            dma((2 + 2 * field_count,)),
             dma,
             dma,
         ],

time: 12.8 us -> 12.1 us (0.945)
  Pallas kernels: 12 us -> 11.3 us
    pallas_call x1, Pallas kernels: 11.3 us -> 10.6 us  [shards(): pl.pallas_call(functools.partial(kernel, sizes), out_shape=(pltpu.VMEM(fi...]
where the time goes in v4:
time: 12.1 us; the launch traced here: 11.9 us
  Pallas kernels  11.3 us (93%)
  between operations  0.64 us (5%)
    pallas_call x1, Pallas kernels, shards(): pl.pallas_call(functools.partial(kernel, sizes), out_shape=(pltpu.VMEM(fi...  10.6 us
    pallas_call x1, Pallas kernels, shards(): pl.pallas_call(put, out_shape=(jax.ShapeDtypeStruct(fields.shape, jnp.flo...  0.66 us

profile of v4, /device:TPU:1, one launch (start us, length us, event | category | flops | bytes accessed | tf_op | source)
XLA Modules:
  0.0 11.9 jit_solution(398729930308809286)
XLA Ops:
  0.6 10.6 %shard_map.50 = (f32[5,16,256]{2,1,0:T(8,128)S(1)}, f32[5]{0:T(128)S(1)}) custom-call(f32[5,16,256]{2,1,0:T(8,128)} %fields_ref.1, s32[16,256]{1,0:T(8,128)} %cell_ref.1, f32[16,256]{1,0:T(8,128)} %frac_ref.1), custom_call_target="tpu_custom_call" | custom-call | tf_op jit(solution)/shard_map/pallas_call | solution.py:216
  11.3 0.7 %shard_map.51 = (f32[5,16,256]{2,1,0:T(8,128)}, f32[5]{0:T(128)}) custom-call(f32[5,16,256]{2,1,0:T(8,128)S(1)} %get-tuple-element.4.new_ref, f32[5]{0:T(128)S(1)} %get-tuple-element.5.mean_ref), custom_call_target="tpu_custom_call" | custom-call | tf_op jit(solution)/shard_map/pallas_call | solution.py:240

commit v5 on v4

--- a/solution.py
+++ b/solution.py
@@ -110,8 +110,10 @@
             device_id=who, device_id_type=MESH,
         ).start()
 
+    for copy in copies[:2]:
+        copy.start()
     others(send)
-    for copy in copies:
+    for copy in copies[2:]:
         copy.start()
     for copy in copies[:2]:
         copy.wait_recv()

time: 12.1 us -> 12.2 us (level)
    pallas_call x1, Pallas kernels: 10.6 us -> 10.8 us  [shards(): pl.pallas_call(functools.partial(kernel, sizes), out_shape=(pltpu.VMEM(fi...]
where the time goes in v5:
time: 12.2 us; the launch traced here: 12.1 us
  Pallas kernels  11.4 us (93%)
  between operations  0.64 us (5%)
    pallas_call x1, Pallas kernels, shards(): pl.pallas_call(functools.partial(kernel, sizes), out_shape=(pltpu.VMEM(fi...  10.8 us
    pallas_call x1, Pallas kernels, shards(): pl.pallas_call(put, out_shape=(jax.ShapeDtypeStruct(fields.shape, jnp.flo...  0.66 us

profile of v5, /device:TPU:1, one launch (start us, length us, event | category | flops | bytes accessed | tf_op | source)
XLA Modules:
  0.0 12.1 jit_solution(6440946762279301210)
XLA Ops:
  0.6 10.8 %shard_map.50 = (f32[5,16,256]{2,1,0:T(8,128)S(1)}, f32[5]{0:T(128)S(1)}) custom-call(f32[5,16,256]{2,1,0:T(8,128)} %fields_ref.1, s32[16,256]{1,0:T(8,128)} %cell_ref.1, f32[16,256]{1,0:T(8,128)} %frac_ref.1), custom_call_target="tpu_custom_call" | custom-call | tf_op jit(solution)/shard_map/pallas_call | solution.py:218
  11.4 0.7 %shard_map.51 = (f32[5,16,256]{2,1,0:T(8,128)}, f32[5]{0:T(128)}) custom-call(f32[5,16,256]{2,1,0:T(8,128)S(1)} %get-tuple-element.4.new_ref, f32[5]{0:T(128)S(1)} %get-tuple-element.5.mean_ref), custom_call_target="tpu_custom_call" | custom-call | tf_op jit(solution)/shard_map/pallas_call | solution.py:242
